TPU v7x, 32 devices: a whole 2x2x4 slice. The times are simulated.
32 devices in a mesh: seq: 8 (over y, x, core), head: 4 (over z).
Axes of the slice: x: 2, y: 2, z: 4, core: 2. Of those that a mesh axis runs over, the one named last changes fastest.
Arguments:
- tokens: bfloat16 [32768, 512], P(('seq', 'head')), may hold values from -8.4 to 8.4
- cotangent: bfloat16 [32768, 512], P(('seq', 'head')), may hold values from -6 to 6
- w_qkv: bfloat16 [512, 1536], P(('seq', 'head')), may hold values from -0.25 to 0.25
- w_out: bfloat16 [512, 512], P(('seq', 'head')), may hold values from -0.5 to 0.5
- w_up: bfloat16 [512, 2048], P(None, ('seq', 'head')), may hold values from -0.25 to 0.25
- w_down: bfloat16 [2048, 512], P(('seq', 'head')), may hold values from -0.1875 to 0.1875
- gain_one: bfloat16 [512], P(('seq', 'head')), may hold values from 0.099609375 to 1.8984375
- shift_one: bfloat16 [512], P(('seq', 'head')), may hold values from -1.5 to 1.5
- gain_two: bfloat16 [512], P(('seq', 'head')), may hold values from 0.099609375 to 1.8984375
- shift_two: bfloat16 [512], P(('seq', 'head')), may hold values from -1.5 to 1.5
- span_doc: int32 [128], replicated, may hold values from 0 to 15, never falling along the last dimension, each value on 1 to 16 neighbouring positions
Outputs:
- out_tokens: bfloat16 [32768, 512], P(('seq', 'head'))
- d_tokens: float32 [32768, 512], P(('seq', 'head'))
- d_w_qkv: float32 [512, 1536], P(('seq', 'head'))
- d_w_out: float32 [512, 512], P(('seq', 'head'))
- d_w_up: float32 [512, 2048], P(None, ('seq', 'head'))
- d_w_down: float32 [2048, 512], P(('seq', 'head'))
- d_gain_one: float32 [512], P(('seq', 'head'))
- d_shift_one: float32 [512], P(('seq', 'head'))
- d_gain_two: float32 [512], P(('seq', 'head'))
- d_shift_two: float32 [512], P(('seq', 'head'))
Inputs may be any that keep to these rules, and one draw needn't show every extreme that they name: span_doc[j] is the document of continuation span j; the numbers never fall along j, every continuation holds 1 to 16 spans, and one holds exactly 16.
All inputs are finite; a program needn't handle non-finite values.
Results may differ from a plain program's by a relative error of at most 0.012.
Values may be sent and summed in bfloat16 or wider, within the bound.
A program may use at most 128 MiB of HBM per device.

v0:
```python
import math
import jax
import jax.numpy as jnp
from jax import lax
from jax.sharding import PartitionSpec as P

H = 8
HD = 64
S = 128
QB = 512
MOST = 16
PSPANS = 128
epsilon = 1e-05
masked_score = -1e30


def layer_norm(values, gain, shift):
    row_mean = jnp.mean(values, axis=-1, keepdims=True)
    centred = values - row_mean
    variance = jnp.mean(centred * centred, axis=-1, keepdims=True)
    return centred * lax.rsqrt(variance + epsilon) * gain + shift


def gelu_tanh(values):
    return jax.nn.gelu(values, approximate=True)


def window_rows(first_span, sum_keys_all, sum_vals_all, docs_all):
    spans_blk = QB // S
    window = MOST + spans_blk
    win_start = jnp.maximum(first_span - MOST, 0)
    win_keys = lax.dynamic_slice_in_dim(sum_keys_all, win_start, window, 0)
    win_vals = lax.dynamic_slice_in_dim(sum_vals_all, win_start, window, 0)
    win_docs = lax.dynamic_slice_in_dim(docs_all, win_start, window, 0)
    sum_keys = jnp.concatenate([sum_keys_all[:PSPANS], win_keys], axis=0)
    sum_vals = jnp.concatenate([sum_vals_all[:PSPANS], win_vals], axis=0)
    sum_index = jnp.concatenate(
        [jnp.arange(PSPANS, dtype=jnp.int32), win_start + jnp.arange(window, dtype=jnp.int32)]
    )
    row_docs = jnp.concatenate([jnp.full((PSPANS,), -2, jnp.int32), win_docs])
    prompt_row = jnp.arange(PSPANS + window) < PSPANS
    query_span = first_span + jnp.arange(spans_blk, dtype=jnp.int32)
    query_doc = lax.dynamic_slice_in_dim(docs_all, first_span, spans_blk, 0)
    earlier = sum_index[None, :] < query_span[:, None]
    same_doc = (sum_index[None, :] >= PSPANS) & (row_docs[None, :] == query_doc[:, None])
    allowed = (earlier & (prompt_row[None, :] | same_doc))[:, None, :]
    return (sum_keys, sum_vals, allowed, win_start)


def block_logits(q_spans, k_blk, sum_keys, allowed):
    score_scale = 1.0 / math.sqrt(HD)
    direct = (
        jnp.einsum("nihe,njhe->hnij", q_spans, k_blk, preferred_element_type=jnp.float32)
        * score_scale
    )
    causal = jnp.arange(S)[:, None] >= jnp.arange(S)[None, :]
    direct = jnp.where(causal, direct, masked_score)
    summary = (
        jnp.einsum("nihe,the->hnit", q_spans, sum_keys, preferred_element_type=jnp.float32)
        * score_scale
    )
    summary = jnp.where(allowed, summary, masked_score)
    return (direct, summary)


def shards(
    tokens,
    cotangent,
    w_qkv,
    w_out,
    w_up,
    w_down,
    gain_one,
    shift_one,
    gain_two,
    shift_two,
    span_doc,
):
    seq_count = lax.axis_size("seq")
    head_count = lax.axis_size("head")
    tok_rows = tokens.shape[0]
    spans_blk = QB // S
    score_scale = 1.0 / math.sqrt(HD)
    grad_scale = 1.0 / math.sqrt(tok_rows * seq_count * head_count)
    docs_all = jnp.concatenate([jnp.full((PSPANS,), -1, jnp.int32), span_doc])
    qkv_mat, out_mat, up_mat, down_mat, gone_full, sone_full, gtwo_full, stwo_full = (
        lax.all_gather(w_qkv, ("seq", "head"), axis=0, tiled=True),
        lax.all_gather(w_out, ("seq", "head"), axis=0, tiled=True),
        lax.all_gather(w_up, ("seq", "head"), axis=1, tiled=True),
        lax.all_gather(w_down, ("seq", "head"), axis=0, tiled=True),
        lax.all_gather(gain_one, ("seq", "head"), axis=0, tiled=True),
        lax.all_gather(shift_one, ("seq", "head"), axis=0, tiled=True),
        lax.all_gather(gain_two, ("seq", "head"), axis=0, tiled=True),
        lax.all_gather(shift_two, ("seq", "head"), axis=0, tiled=True),
    )
    gone_full = gone_full.astype(jnp.float32)
    sone_full = sone_full.astype(jnp.float32)
    gtwo_full = gtwo_full.astype(jnp.float32)
    stwo_full = stwo_full.astype(jnp.float32)
    x_rows = tokens.astype(jnp.float32)
    norm_one, back_one = jax.vjp(layer_norm, x_rows, gone_full, sone_full)
    act_one = norm_one.astype(jnp.bfloat16)
    qkv_rows = jnp.dot(act_one, qkv_mat, preferred_element_type=jnp.float32).astype(jnp.bfloat16)
    heads_dev = H // head_count
    tok_grp = tok_rows * head_count
    group_index = lax.axis_index("seq")
    qkv_local = lax.all_to_all(qkv_rows, "head", split_axis=1, concat_axis=0, tiled=True)
    spans_grp = tok_grp // S
    all_spans = spans_grp * seq_count
    block_count = tok_grp // QB
    grouped = qkv_local.reshape(tok_grp, heads_dev, 3, HD)
    pair_part = grouped[:, :, 1:].reshape(spans_grp, S, heads_dev * 2 * HD)
    span_kv = (jnp.sum(pair_part, axis=1, dtype=jnp.float32) / S).astype(jnp.bfloat16)
    all_kv = lax.all_gather(span_kv, "seq", axis=0, tiled=True)
    all_kv = all_kv.reshape(all_spans, heads_dev, 2, HD)
    sum_keys_all = all_kv[:, :, 0]
    sum_vals_all = all_kv[:, :, 1]
    block_ids = jnp.arange(block_count, dtype=jnp.int32)
    q_blocks = grouped[:, :, 0].reshape(block_count, spans_blk, S, heads_dev, HD)
    k_blocks = grouped[:, :, 1].reshape(block_count, spans_blk, S, heads_dev, HD)
    v_blocks = grouped[:, :, 2].reshape(block_count, spans_blk, S, heads_dev, HD)

    def forward_block(inputs):
        block_id, q_spans, k_blk, v_blk = inputs
        first_span = group_index * spans_grp + block_id * spans_blk
        sum_keys, sum_vals, allowed, win_start = window_rows(
            first_span, sum_keys_all, sum_vals_all, docs_all
        )
        direct, summary = block_logits(q_spans, k_blk, sum_keys, allowed)
        row_top = jnp.maximum(jnp.max(direct, axis=-1), jnp.max(summary, axis=-1))
        exp_dir = jnp.exp(direct - row_top[..., None])
        exp_sum = jnp.exp(summary - row_top[..., None])
        denominator = jnp.sum(exp_dir, axis=-1) + jnp.sum(exp_sum, axis=-1)
        low_dir = (exp_dir / denominator[..., None]).astype(jnp.bfloat16)
        lower_total_sum = (exp_sum / denominator[..., None]).astype(jnp.bfloat16)
        mixed_rows = jnp.einsum(
            "hnij,njhe->nihe", low_dir, v_blk, preferred_element_type=jnp.float32
        )
        mixed_rows = mixed_rows + jnp.einsum(
            "hnit,the->nihe", lower_total_sum, sum_vals, preferred_element_type=jnp.float32
        )
        return (
            mixed_rows.astype(jnp.bfloat16).reshape(QB, heads_dev * HD),
            row_top + jnp.log(denominator),
        )

    local_attention, log_totals = lax.map(forward_block, (block_ids, q_blocks, k_blocks, v_blocks))
    local_attention = local_attention.reshape(tok_grp, heads_dev * HD)
    attn_rows = lax.all_to_all(local_attention, "head", split_axis=0, concat_axis=1, tiled=True)
    resid = x_rows + jnp.dot(attn_rows, out_mat, preferred_element_type=jnp.float32)
    norm_two, back_two = jax.vjp(layer_norm, resid, gtwo_full, stwo_full)
    act_two = norm_two.astype(jnp.bfloat16)
    hidden = jnp.dot(act_two, up_mat, preferred_element_type=jnp.float32)
    acted, back_gelu = jax.vjp(gelu_tanh, hidden)
    acted_low = acted.astype(jnp.bfloat16)
    out_rows = resid + jnp.dot(acted_low, down_mat, preferred_element_type=jnp.float32)
    d_acted = jnp.dot(cotangent, down_mat.T, preferred_element_type=jnp.float32)
    d_hidden = back_gelu(d_acted)[0].astype(jnp.bfloat16)
    grad_down = jnp.dot(acted_low.T, cotangent, preferred_element_type=jnp.float32)
    grad_up = jnp.dot(act_two.T, d_hidden, preferred_element_type=jnp.float32)
    d_norm_two = jnp.dot(d_hidden, up_mat.T, preferred_element_type=jnp.float32)
    out_tokens = out_rows.astype(jnp.bfloat16)
    d_resid_norm, grad_gain_two, grad_shift_two = back_two(d_norm_two)
    d_resid = cotangent.astype(jnp.float32) + d_resid_norm
    d_branch = d_resid.astype(jnp.bfloat16)
    grad_out = jnp.dot(attn_rows.T, d_branch, preferred_element_type=jnp.float32)
    d_attn = jnp.dot(d_branch, out_mat.T, preferred_element_type=jnp.float32).astype(jnp.bfloat16)
    local_gradient = lax.all_to_all(d_attn, "head", split_axis=1, concat_axis=0, tiled=True)
    do_blocks = local_gradient.reshape(block_count, spans_blk, S, heads_dev, HD)

    def backward_block(sum_grads, inputs):
        block_id, q_spans, k_blk, v_blk, output_span_gradient, log_blk = inputs
        first_span = group_index * spans_grp + block_id * spans_blk
        sum_keys, sum_vals, allowed, win_start = window_rows(
            first_span, sum_keys_all, sum_vals_all, docs_all
        )
        direct, summary = block_logits(q_spans, k_blk, sum_keys, allowed)
        prob_dir = jnp.exp(direct - log_blk[..., None])
        prob_sum = jnp.exp(summary - log_blk[..., None])
        low_dir = prob_dir.astype(jnp.bfloat16)
        lower_total_sum = prob_sum.astype(jnp.bfloat16)
        grad_dir = jnp.einsum(
            "nihe,njhe->hnij", output_span_gradient, v_blk, preferred_element_type=jnp.float32
        )
        grad_sum = jnp.einsum(
            "nihe,the->hnit", output_span_gradient, sum_vals, preferred_element_type=jnp.float32
        )
        delta = jnp.sum(prob_dir * grad_dir, axis=-1) + jnp.sum(prob_sum * grad_sum, axis=-1)
        ds_dir = (prob_dir * (grad_dir - delta[..., None])).astype(jnp.bfloat16)
        ds_sum = (prob_sum * (grad_sum - delta[..., None])).astype(jnp.bfloat16)
        d_query = jnp.einsum("hnij,njhe->nihe", ds_dir, k_blk, preferred_element_type=jnp.float32)
        d_query = (
            d_query
            + jnp.einsum("hnit,the->nihe", ds_sum, sum_keys, preferred_element_type=jnp.float32)
        ) * score_scale
        d_key = (
            jnp.einsum("hnij,nihe->njhe", ds_dir, q_spans, preferred_element_type=jnp.float32)
            * score_scale
        )
        d_value = jnp.einsum(
            "hnij,nihe->njhe", low_dir, output_span_gradient, preferred_element_type=jnp.float32
        )
        summary_key_gradient = (
            jnp.einsum("kord,orkj->dkj", ds_sum, q_spans, preferred_element_type=jnp.float32)
            * score_scale
        )
        summary_value_gradient = jnp.einsum(
            "kord,orkj->dkj",
            lower_total_sum,
            output_span_gradient,
            preferred_element_type=jnp.float32,
        )
        paired_gradient = jnp.stack([summary_key_gradient, summary_value_gradient], axis=2)
        sum_grads = sum_grads.at[:PSPANS].add(paired_gradient[:PSPANS])
        current = lax.dynamic_slice_in_dim(sum_grads, win_start, MOST + spans_blk, 0)
        sum_grads = lax.dynamic_update_slice_in_dim(
            sum_grads, current + paired_gradient[PSPANS:], win_start, 0
        )
        return (sum_grads, (d_query, d_key, d_value))

    start_grads = jnp.zeros((all_spans, heads_dev, 2, HD), jnp.float32)
    sum_grads, (dq_blocks, dk_blocks, dv_blocks) = lax.scan(
        backward_block,
        start_grads,
        (block_ids, q_blocks, k_blocks, v_blocks, do_blocks, log_totals),
    )
    flat_grads = sum_grads.reshape(all_spans, heads_dev * 2 * HD)
    span_grads = lax.psum_scatter(
        flat_grads.astype(jnp.bfloat16), "seq", scatter_dimension=0, tiled=True
    ).astype(jnp.float32)
    span_grads = span_grads.reshape(spans_grp, 1, heads_dev, 2, HD) / S
    d_key_all = dk_blocks.reshape(spans_grp, S, heads_dev, HD) + span_grads[:, :, :, 0]
    d_val_all = dv_blocks.reshape(spans_grp, S, heads_dev, HD) + span_grads[:, :, :, 1]
    d_qkv_local = jnp.stack(
        [
            dq_blocks.reshape(tok_grp, heads_dev, HD),
            d_key_all.reshape(tok_grp, heads_dev, HD),
            d_val_all.reshape(tok_grp, heads_dev, HD),
        ],
        axis=2,
    )
    d_qkv_local = d_qkv_local.astype(jnp.bfloat16).reshape(tok_grp, heads_dev * 3 * HD)
    d_qkv_rows = lax.all_to_all(d_qkv_local, "head", split_axis=0, concat_axis=1, tiled=True)
    grad_qkv = jnp.dot(act_one.T, d_qkv_rows, preferred_element_type=jnp.float32)
    d_norm_one = jnp.dot(d_qkv_rows, qkv_mat.T, preferred_element_type=jnp.float32)
    d_x_norm, grad_gain_one, first_shift_gradient = back_one(d_norm_one)
    d_tokens = d_resid + d_x_norm
    (
        grad_qkv,
        grad_out,
        grad_up,
        grad_down,
        grad_gain_one,
        first_shift_gradient,
        grad_gain_two,
        grad_shift_two,
    ) = (
        lax.psum_scatter(grad_qkv, ("seq", "head"), scatter_dimension=0, tiled=True),
        lax.psum_scatter(grad_out, ("seq", "head"), scatter_dimension=0, tiled=True),
        lax.psum_scatter(grad_up, ("seq", "head"), scatter_dimension=1, tiled=True),
        lax.psum_scatter(grad_down, ("seq", "head"), scatter_dimension=0, tiled=True),
        lax.psum_scatter(grad_gain_one, ("seq", "head"), scatter_dimension=0, tiled=True),
        lax.psum_scatter(first_shift_gradient, ("seq", "head"), scatter_dimension=0, tiled=True),
        lax.psum_scatter(grad_gain_two, ("seq", "head"), scatter_dimension=0, tiled=True),
        lax.psum_scatter(grad_shift_two, ("seq", "head"), scatter_dimension=0, tiled=True),
    )
    return (
        out_tokens,
        d_tokens,
        grad_qkv * grad_scale,
        grad_out * grad_scale,
        grad_up * grad_scale,
        grad_down * grad_scale,
        grad_gain_one * grad_scale,
        first_shift_gradient * grad_scale,
        grad_gain_two * grad_scale,
        grad_shift_two * grad_scale,
    )


def solution(mesh):
    in_specs = (
        P(("seq", "head"), None),
        P(("seq", "head"), None),
        P(("seq", "head"), None),
        P(("seq", "head"), None),
        P(None, ("seq", "head")),
        P(("seq", "head"), None),
        P(("seq", "head")),
        P(("seq", "head")),
        P(("seq", "head")),
        P(("seq", "head")),
        P(),
    )
    out_specs = (
        P(("seq", "head"), None),
        P(("seq", "head"), None),
        P(("seq", "head"), None),
        P(("seq", "head"), None),
        P(None, ("seq", "head")),
        P(("seq", "head"), None),
        P(("seq", "head")),
        P(("seq", "head")),
        P(("seq", "head")),
        P(("seq", "head")),
    )
    return jax.shard_map(shards, mesh=mesh, in_specs=in_specs, out_specs=out_specs, check_vma=False)
```

profile of v0, /device:TPU:0, one launch (start us, length us, event | category | flops | bytes accessed | tf_op | source)
XLA Modules:
  0.0 1173.3 jit_solution(1539304039287238738)
XLA Ops:
  11.3 42.1 %all-reduce.12 = (bf16[512]{0:T(512)(128)(2,1)S(1)}, bf16[512]{0:T(512)(128)(2,1)S(1)}, bf16[512]{0:T(512)(128)(2,1)}, bf16[512]{0:T(512)(128)(2,1)}) all-reduce(bf16[512]{0:T(512)(128)(2,1)S(1)} %dynamic-update-slice.7, bf16[512]{0:T(512)(128)(2,1)S(1)} %dynamic-update-slice.6, ...), channel_id=1, replica_groups=mesh['seq'=8,'head'=4] {'seq','head'}, use_global_device_ids=true, to_apply=%add.4 | all-reduce | flops 2048 | bytes 8192
  56.0 12.7 %all-gather.4.cloned.1.call-done = bf16[512,1536]{1,0:T(8,128)(2,1)} async-done(((bf16[16,1536]{1,0:T(8,128)(2,1)}), bf16[512,1536]{1,0:T(8,128)(2,1)}) %all-gather.4.cloned.1.call-update) | async-done | bytes 1572880 | tf_op jit(solution)/shard_map/all_gather | solution.py:87
  68.7 5.1 convolution_convert_fusion
  73.8 4.6 copy.204
  78.4 4.8 all-to-all-start
  84.8 74.1 %all-to-all-done = bf16[1024,4,384]{0,2,1:T(8,128)(2,1)} async-done(((bf16[1024,4,384]{0,2,1:T(8,128)(2,1)}), bf16[1024,4,384]{0,2,1:T(8,128)(2,1)}, u32[]{:S(2)}, u32[]{:S(2)}) %all-to-all-start) | async-done | bytes 3145760 | tf_op jit(solution)/shard_map/all_to_all | solution.py:107
  158.9 6.0 copy.163
  164.9 6.1 reshape.339
  184.1 4.9 copy.232
  192.5 9.2 all_gather.30
  202.9 68.9 %while.33 = (s32[]{:T(128)}, bf16[8,512,128]{2,1,0:T(8,128)(2,1)}, f32[8,2,4,128]{3,2,1,0:T(4,128)}, bf16[8,4,128,2,64]{2,1,0,4,3:T(4,128)(2,1)}, bf16[8,4,128,2...) while((s32[]{:T(128)}, bf16[8,512,128]{2,1,0:T(8,128)(2,1)}, ...), condition=%wide.region_8.9_spmd, body=%wide.region_3.8_spmd.sunk | while | flops 74914296 | bytes 5989179 | solution.py:147
  271.9 4.4 all-to-all-start.1
  279.2 90.4 %all_gather.31 = bf16[512,512]{1,0:T(8,128)(2,1)} all-gather(bf16[16,512]{1,0:T(8,128)(2,1)S(1)} %copy-done.18), channel_id=1, replica_groups=mesh['seq'=8,'head'=4] {'seq','head'}, dimensions={0}, use_global_device_ids=true | all-gather | bytes 540672 | tf_op jit(solution)/shard_map/all_gather | solution.py:88
  374.6 7.6 fusion.83
  382.2 9.7 fusion.63
  408.6 20.8 %all-to-all-done.2 = bf16[1024,4,128]{0,2,1:T(8,128)(2,1)S(1)} async-done(((bf16[1024,4,128]{0,2,1:T(8,128)(2,1)}), bf16[1024,4,128]{0,2,1:T(8,128)(2,1)S(1)}, u32[]{:S(2)}, u32[]{:S(2)}) %all-to-all-start.2) | async-done | bytes 1048608 | tf_op jit(solution)/shard_map/all_to_all | solution.py:168
  433.5 120.3 %while.34 = (s32[]{:T(128)}, f32[256,2,2,64]{0,3,1,2:T(8,128)S(1)}, bf16[8,4,128,2,64]{2,4,3,1,0:T(8,128)(2,1)}, f32[8,4,128,2,64]{2,1,0,4,3:T(4,128)}, f32[8,4,...) while((s32[]{:T(128)}, f32[256,2,2,64]{0,3,1,2:T(8,128)S(1)}, ...), condition=%wide.region_16.17_spmd, body=%wide.region_13.16_spmd.sunk | while | flops 183960576 | bytes 14116731 | solution.py:222
  558.1 9.1 fusion.84
  568.8 6.7 fusion.82
  598.2 4.1 add_convert_fusion
  604.7 6.2 convert_element_type.128
  610.9 4.6 copy.184
  615.5 4.8 all-to-all-start.3
  620.5 76.7 %all-to-all-done.3 = bf16[4,1024,384]{1,2,0:T(8,128)(2,1)} async-done(((bf16[4,1024,384]{1,2,0:T(8,128)(2,1)}), bf16[4,1024,384]{1,2,0:T(8,128)(2,1)}, u32[]{:S(2)}, u32[]{:S(2)}) %all-to-all-start.3) | async-done | bytes 3145760 | tf_op jit(solution)/shard_map/all_to_all | solution.py:243
  697.2 5.6 fusion.79
  702.8 8.4 add_convert_fusion.2
  713.6 45.2 %reduce-scatter.10.cloned.1.call-done = f32[16,512]{1,0:T(8,128)} async-done(((f32[512,512]{1,0:T(8,128)}), f32[16,512]{1,0:T(8,128)}) %reduce-scatter.10.cloned.1.call-update) | async-done | bytes 32784 | tf_op jit(solution)/shard_map/reduce_scatter | solution.py:259
  760.2 5.1 fusion.91
  774.9 40.1 %all-reduce.11 = (f32[512]{0:T(512)S(1)}, f32[512]{0:T(512)S(1)}, f32[512]{0:T(512)S(1)}, f32[512]{0:T(512)S(1)}) all-reduce(f32[512]{0:T(512)S(1)} %get-tuple-element.526, f32[512]{0:T(512)S(1)} %get-tuple-element.617, f32[512]{0:T(512)S(1)} %get-tuple-element.524, ...), channel_id=7, replica_groups=mesh['seq'=8,'head'=4] {'seq','head'}, use_global_device_ids=true, to_apply=%region_25.26.clone | all-reduce | flops 2048 | bytes 16384
  817.3 92.8 %reduce-scatter.14.cloned.1.call-done = f32[64,512]{1,0:T(8,128)} async-done(((f32[2048,512]{1,0:T(8,128)}), f32[64,512]{1,0:T(8,128)}) %reduce-scatter.14.cloned.1.call-update) | async-done | bytes 131088 | tf_op jit(solution)/shard_map/reduce_scatter | solution.py:261
  911.6 147.4 %reduce-scatter.12.cloned.1.call-done = f32[512,64]{0,1:T(8,128)} async-done(((f32[512,2048]{0,1:T(8,128)}), f32[512,64]{0,1:T(8,128)}) %reduce-scatter.12.cloned.1.call-update) | async-done | bytes 131088 | tf_op jit(solution)/shard_map/reduce_scatter | solution.py:260
  1060.6 104.2 %reduce-scatter.8.cloned.1.call-done = f32[16,1536]{1,0:T(8,128)} async-done(((f32[512,1536]{1,0:T(8,128)}), f32[16,1536]{1,0:T(8,128)}) %reduce-scatter.8.cloned.1.call-update) | async-done | bytes 98320 | tf_op jit(solution)/shard_map/reduce_scatter | solution.py:258
  (663 shorter events, 283.3 us)
Async XLA Ops:
  7.2 61.6 %all-gather.4.cloned.1.call-start = ((), (), s32[]{:S(2)}) async-start(), calls=%async_computation.9 | async-start | bytes 1622016 | tf_op jit(solution)/shard_map/all_gather | solution.py:87
  53.4 15.3 %copy-start.19 = (f32[512]{0:T(512)}, f32[512]{0:T(512)S(1)}, u32[]{:S(2)}) copy-start(f32[512]{0:T(512)S(1)} %convert_element_type.110) | copy-start | bytes 6148
  78.4 6.3 copy-start.26
  78.4 80.4 %all-to-all-start = ((bf16[1024,4,384]{0,2,1:T(8,128)(2,1)}), bf16[1024,4,384]{0,2,1:T(8,128)(2,1)}, u32[]{:S(2)}, u32[]{:S(2)}) async-start(bf16[1024,4,384]{0,2,1:T(8,128)(2,1)} %bitcast.293), calls=%async_computation | async-start | bytes 6291456 | tf_op jit(solution)/shard_map/all_to_all | solution.py:107
  83.2 291.0 %all-gather.6.cloned.1.call-start = ((), (), s32[]{:S(2)}) async-start(), calls=%async_computation.10 | async-start | bytes 2162688 | tf_op jit(solution)/shard_map/all_gather | solution.py:89
  84.0 298.2 %all-gather.8.cloned.1.call-start = ((), (), s32[]{:S(2)}) async-start(), calls=%async_computation.11 | async-start | bytes 2162688 | tf_op jit(solution)/shard_map/all_gather | solution.py:90
  171.0 3.6 copy-start.4
  178.2 2.7 copy-start.12
  271.8 4.4 copy-start.24
  271.9 7.3 copy-start.2
  271.9 7.3 copy-start.10
  271.9 4.4 copy-start.23
  271.9 4.5 copy-start.22
  271.9 7.3 copy-start.18
  271.9 97.6 %all-to-all-start.1 = ((bf16[4,1024,128]{2,1,0:T(8,128)(2,1)}), bf16[4,1024,128]{2,1,0:T(8,128)(2,1)}, u32[]{:S(2)}, u32[]{:S(2)}) async-start(bf16[4,1024,128]{2,1,0:T(8,128)(2,1)} %bitcast.297), calls=%async_computation.1 | async-start | bytes 2097152 | tf_op jit(solution)/shard_map/all_to_all | solution.py:149
  373.9 26.9 %copy-start = (f32[1024,512]{0,1:T(8,128)}, f32[1024,512]{0,1:T(8,128)S(1)}, u32[]{:S(2)}) copy-start(f32[1024,512]{0,1:T(8,128)S(1)} %get-tuple-element.616) | copy-start | bytes 6291460
  382.1 9.7 copy-start.27
  391.8 3.7 copy-start.29
  398.4 2.4 copy-start.5
  404.8 24.6 %all-to-all-start.2 = ((bf16[1024,4,128]{0,2,1:T(8,128)(2,1)}), bf16[1024,4,128]{0,2,1:T(8,128)(2,1)S(1)}, u32[]{:S(2)}, u32[]{:S(2)}) async-start(bf16[1024,4,128]{0,2,1:T(8,128)(2,1)} %bitcast.43), calls=%async_computation.2 | async-start | bytes 2097152 | tf_op jit(solution)/shard_map/all_to_all | solution.py:168
  408.4 179.6 %reduce-scatter.16.cloned.1.call-start = ((), (), s32[]{:S(2)}) async-start(), calls=%async_computation.16 | async-start | bytes 147456
  429.4 4.1 copy-start.3
  429.4 4.1 copy-start.25
  554.6 3.5 copy-start.15
  554.6 204.2 %reduce-scatter.10.cloned.1.call-start = ((), (), s32[]{:S(2)}) async-start(), calls=%async_computation.13 | async-start | bytes 1081344 | tf_op jit(solution)/shard_map/reduce_scatter | solution.py:259
  558.0 352.0 %reduce-scatter.14.cloned.1.call-start = ((), (), s32[]{:S(2)}) async-start(), calls=%async_computation.15 | async-start | bytes 4325376 | tf_op jit(solution)/shard_map/reduce_scatter | solution.py:261
  567.2 491.8 %reduce-scatter.12.cloned.1.call-start = ((), (), s32[]{:S(2)}) async-start(), calls=%async_computation.14 | async-start | bytes 4325376 | tf_op jit(solution)/shard_map/reduce_scatter | solution.py:260
  598.2 4.1 copy-start.11
  615.5 81.8 %copy-start.20 = (f32[512]{0:T(512)S(1)}, f32[512]{0:T(512)}, u32[]{:S(2)}) copy-start(f32[512]{0:T(512)} %copy-done.19) | copy-start | bytes 6148
  615.5 81.8 %all-to-all-start.3 = ((bf16[4,1024,384]{1,2,0:T(8,128)(2,1)}), bf16[4,1024,384]{1,2,0:T(8,128)(2,1)}, u32[]{:S(2)}, u32[]{:S(2)}) async-start(bf16[4,1024,384]{1,2,0:T(8,128)(2,1)} %copy.184), calls=%async_computation.3 | async-start | bytes 6291456 | tf_op jit(solution)/shard_map/all_to_all | solution.py:243
  620.3 544.5 %reduce-scatter.8.cloned.1.call-start = ((), (), s32[]{:S(2)}) async-start(), calls=%async_computation.12 | async-start | bytes 3244032 | tf_op jit(solution)/shard_map/reduce_scatter | solution.py:258
  711.2 49.0 %copy-start.28 = (bf16[512,1536]{1,0:T(8,128)(2,1)S(1)}, bf16[512,1536]{1,0:T(8,128)(2,1)}, u32[]{:S(2)}) copy-start(bf16[512,1536]{1,0:T(8,128)(2,1)} %all-gather.4.cloned.1.call-done) | copy-start | bytes 4718596
  (10 other events, 12.3 us)
Sparse Core Ops, SparseCore 0:
  10.9 57.8 all-gather.3
  87.0 90.1 all-gather.5
  180.1 55.4 all-gather.7
  554.7 33.1 reduce-scatter.15
  590.1 168.6 reduce-scatter.9
  760.9 149.0 reduce-scatter.13
  912.3 146.6 reduce-scatter.11
  1064.4 100.2 reduce-scatter.7
where the time goes:
time: 1180 us; the launch traced here: 1170 us
  waiting for transfers between devices  576 us (49%)
  local copies, waits for them, and re-layouts  213 us (18%)
  blocking collectives  182 us (15%)
  matrix products  118 us (10%)
  other arithmetic  37.9 us (3%)
  starting transfers between devices  19.1 us (2%)
  between operations  14.8 us (1%)
  loops' own time  12 us (1%)
    reduce_scatter x1, waiting for transfers between devices, shards(): lax.psum_scatter(grad_up, ('seq', 'head'), scatter_dimension=1, tiled=True)  147 us
    reduce_scatter x1, waiting for transfers between devices, shards(): lax.psum_scatter(grad_qkv, ('seq', 'head'), scatter_dimension=0, tiled=True)  104 us
    reduce_scatter x1, waiting for transfers between devices, shards(): lax.psum_scatter(grad_down, ('seq', 'head'), scatter_dimension=0, tiled=T...  92.8 us
    all_gather x1, blocking collectives, shards(): lax.all_gather(w_out, ('seq', 'head'), axis=0, tiled=True)  90.4 us
    unnamed x2, blocking collectives  82.1 us
    all_to_all x1, waiting for transfers between devices, shards(): lax.all_to_all(d_qkv_local, 'head', split_axis=0, concat_axis=1, tiled=True)  76.7 us
    all_to_all x1, waiting for transfers between devices, shards(): lax.all_to_all(qkv_rows, 'head', split_axis=1, concat_axis=0, tiled=True)  74.1 us
    reduce_scatter x1, waiting for transfers between devices, shards(): lax.psum_scatter(grad_out, ('seq', 'head'), scatter_dimension=0, tiled=True)  45.2 us
  transfers between devices with their start and end apart: 12, of which 9 were waited for; matrix products, arithmetic and copies ran while one was open for 18% of the time, Pallas kernels for 0%

commit v1 on v0

--- a/solution.py
+++ b/solution.py
@@ -3,6 +3,7 @@
 import jax.numpy as jnp
 from jax import lax
 from jax.sharding import PartitionSpec as P
+from jax.lax import axis_index, axis_size, ppermute
 
 H = 8
 HD = 64
@@ -104,7 +105,24 @@
     heads_dev = H // head_count
     tok_grp = tok_rows * head_count
     group_index = lax.axis_index("seq")
-    qkv_local = lax.all_to_all(qkv_rows, "head", split_axis=1, concat_axis=0, tiled=True)
+    raw_out = axis_size("head")
+    e_next, outer = (raw_out, axis_index("head"))
+    state_now = qkv_rows.shape[1] // e_next
+    back = list(qkv_rows.shape)
+    back[1] = state_now
+    main = back[0]
+    back[0] = main * e_next
+    qkv_local = jnp.zeros(back, qkv_rows.dtype)
+    for d in range(e_next):
+        frame_out = lax.dynamic_slice_in_dim(qkv_rows, (outer ^ d) * state_now, state_now, axis=1)
+        if d:
+            grid = []
+            for rr in range(e_next):
+                grid.append((rr, rr ^ d))
+            frame_out = ppermute(frame_out, "head", grid)
+        qkv_local = lax.dynamic_update_slice_in_dim(
+            qkv_local, frame_out, (outer ^ d) * main, axis=0
+        )
     spans_grp = tok_grp // S
     all_spans = spans_grp * seq_count
     block_count = tok_grp // QB

time: 1180 us -> 1170 us (level)
  waiting for transfers between devices: 576 us -> 546 us
  starting transfers between devices: 19.1 us -> 38.5 us
    all_to_all x1 -> x0, waiting for transfers between devices: 74.1 us -> none  [shards(): lax.all_to_all(qkv_rows, 'head', split_axis=1, concat_axis=0, tiled=True)]
    ppermute x0 -> x3, waiting for transfers between devices: none -> 44.7 us  [shards(): frame_out = ppermute(frame_out, 'head', grid)]
    all_to_all x1, starting transfers between devices: 4.4 us -> 24.7 us  [shards(): lax.all_to_all(local_attention, 'head', split_axis=0, concat_axis=1, tile...]
    unnamed x75 -> x73, local copies, waits for them, and re-layouts: 23.6 us -> 23.7 us
  transfers between devices with their start and end apart: 12 -> 14, of which waited for: 9 -> 10; matrix products, arithmetic and copies ran while one was open for 18% -> 19% of each run, Pallas kernels for 0% -> 0%
where the time goes in v1:
time: 1170 us; the launch traced here: 1150 us
  waiting for transfers between devices  546 us (47%)
  local copies, waits for them, and re-layouts  207 us (18%)
  blocking collectives  180 us (15%)
  matrix products  116 us (10%)
  other arithmetic  39.6 us (3%)
  starting transfers between devices  38.5 us (3%)
  between operations  14.9 us (1%)
  loops' own time  12 us (1%)
    reduce_scatter x1, waiting for transfers between devices, shards(): lax.psum_scatter(grad_up, ('seq', 'head'), scatter_dimension=1, tiled=True)  147 us
    reduce_scatter x1, waiting for transfers between devices, shards(): lax.psum_scatter(grad_qkv, ('seq', 'head'), scatter_dimension=0, tiled=True)  104 us
    reduce_scatter x1, waiting for transfers between devices, shards(): lax.psum_scatter(grad_down, ('seq', 'head'), scatter_dimension=0, tiled=T...  92.1 us
    all_gather x1, blocking collectives, shards(): lax.all_gather(w_out, ('seq', 'head'), axis=0, tiled=True)  90.7 us
    unnamed x2, blocking collectives  80.3 us
    all_to_all x1, waiting for transfers between devices, shards(): lax.all_to_all(d_qkv_local, 'head', split_axis=0, concat_axis=1, tiled=True)  76.9 us
    reduce_scatter x1, waiting for transfers between devices, shards(): lax.psum_scatter(grad_out, ('seq', 'head'), scatter_dimension=0, tiled=True)  46.2 us
    ppermute x3, waiting for transfers between devices, shards(): frame_out = ppermute(frame_out, 'head', grid)  44.7 us
  transfers between devices with their start and end apart: 14, of which 10 were waited for; matrix products, arithmetic and copies ran while one was open for 19% of the time, Pallas kernels for 0%

profile of v1, /device:TPU:0, one launch (start us, length us, event | category | flops | bytes accessed | tf_op | source)
XLA Modules:
  0.0 1154.7 jit_solution(8404542834195029461)
XLA Ops:
  12.1 42.1 %all-reduce.12 = (bf16[512]{0:T(512)(128)(2,1)S(1)}, bf16[512]{0:T(512)(128)(2,1)S(1)}, bf16[512]{0:T(512)(128)(2,1)}, bf16[512]{0:T(512)(128)(2,1)}) all-reduce(bf16[512]{0:T(512)(128)(2,1)S(1)} %dynamic-update-slice.7, bf16[512]{0:T(512)(128)(2,1)S(1)} %dynamic-update-slice.6, ...), channel_id=1, replica_groups=mesh['seq'=8,'head'=4] {'seq','head'}, use_global_device_ids=true, to_apply=%add.4 | all-reduce | flops 2048 | bytes 8192
  56.9 11.8 %all-gather.4.cloned.1.call-done = bf16[512,1536]{1,0:T(8,128)(2,1)} async-done(((bf16[16,1536]{1,0:T(8,128)(2,1)}), bf16[512,1536]{1,0:T(8,128)(2,1)}) %all-gather.4.cloned.1.call-update) | async-done | bytes 1572880 | tf_op jit(solution)/shard_map/all_gather | solution.py:88
  81.4 32.1 %collective-permute-done.1 = bf16[1024,384]{1,0:T(8,128)(2,1)} collective-permute-done((bf16[1024,384]{1,0:T(8,128)(2,1)}, bf16[1024,384]{1,0:T(8,128)(2,1)}, u32[]{:S(2)}, u32[]{:S(2)}) %collective-permute-start.1) | collective-permute-done | bytes 786464 | tf_op jit(solution)/shard_map/ppermute | solution.py:122
  118.3 12.7 %collective-permute-done.2 = bf16[1024,384]{1,0:T(8,128)(2,1)S(1)} collective-permute-done((bf16[1024,384]{1,0:T(8,128)(2,1)}, bf16[1024,384]{1,0:T(8,128)(2,1)S(1)}, u32[]{:S(2)}, u32[]{:S(2)}) %collective-permute-start.2) | collective-permute-done | bytes 786464 | tf_op jit(solution)/shard_map/ppermute | solution.py:122
  132.2 3.5 fusion.89
  135.7 4.0 slice_convert_fusion
  146.8 4.9 copy.241
  155.2 9.3 all_gather.30
  165.9 68.9 %while.33 = (s32[]{:T(128)}, bf16[8,512,128]{2,1,0:T(8,128)(2,1)}, f32[8,2,4,128]{3,2,1,0:T(4,128)}, bf16[8,4,128,2,64]{2,1,0,4,3:T(4,128)(2,1)}, bf16[8,4,128,2...) while((s32[]{:T(128)}, bf16[8,512,128]{2,1,0:T(8,128)(2,1)}, ...), condition=%wide.region_8.9_spmd, body=%wide.region_3.8_spmd.sunk | while | flops 74914296 | bytes 5989179 | solution.py:165
  234.8 24.7 %all-to-all-start = ((bf16[4,1024,128]{2,1,0:T(8,128)(2,1)}), bf16[4,1024,128]{2,1,0:T(8,128)(2,1)}, u32[]{:S(2)}, u32[]{:S(2)}) async-start(bf16[4,1024,128]{2,1,0:T(8,128)(2,1)} %bitcast.293), calls=%async_computation | async-start | bytes 2097152 | tf_op jit(solution)/shard_map/all_to_all | solution.py:167
  262.4 90.7 %all_gather.31 = bf16[512,512]{1,0:T(8,128)(2,1)} all-gather(bf16[16,512]{1,0:T(8,128)(2,1)S(1)} %copy-done.17), channel_id=1, replica_groups=mesh['seq'=8,'head'=4] {'seq','head'}, dimensions={0}, use_global_device_ids=true | all-gather | bytes 540672 | tf_op jit(solution)/shard_map/all_gather | solution.py:89
  358.2 7.6 fusion.83
  365.7 9.7 fusion.63
  375.4 3.6 fusion.92
  388.4 3.5 all-to-all-start.1
  392.2 20.8 %all-to-all-done.1 = bf16[1024,4,128]{0,2,1:T(8,128)(2,1)S(1)} async-done(((bf16[1024,4,128]{0,2,1:T(8,128)(2,1)}), bf16[1024,4,128]{0,2,1:T(8,128)(2,1)S(1)}, u32[]{:S(2)}, u32[]{:S(2)}) %all-to-all-start.1) | async-done | bytes 1048608 | tf_op jit(solution)/shard_map/all_to_all | solution.py:186
  417.0 120.3 %while.34 = (s32[]{:T(128)}, f32[256,2,2,64]{0,3,1,2:T(8,128)S(1)}, bf16[8,4,128,2,64]{2,4,3,1,0:T(8,128)(2,1)}, f32[8,4,128,2,64]{2,1,0,4,3:T(4,128)}, f32[8,4,...) while((s32[]{:T(128)}, f32[256,2,2,64]{0,3,1,2:T(8,128)S(1)}, ...), condition=%wide.region_16.17_spmd, body=%wide.region_13.16_spmd.sunk | while | flops 183960576 | bytes 14116731 | solution.py:240
  541.6 9.1 fusion.84
  552.3 6.7 fusion.82
  581.8 4.1 add_convert_fusion
  588.2 6.2 convert_element_type.128
  594.4 4.6 copy.194
  599.0 4.8 all-to-all-start.2
  604.0 76.9 %all-to-all-done.2 = bf16[4,1024,384]{1,2,0:T(8,128)(2,1)} async-done(((bf16[4,1024,384]{1,2,0:T(8,128)(2,1)}), bf16[4,1024,384]{1,2,0:T(8,128)(2,1)}, u32[]{:S(2)}, u32[]{:S(2)}) %all-to-all-start.2) | async-done | bytes 3145760 | tf_op jit(solution)/shard_map/all_to_all | solution.py:261
  680.9 5.6 fusion.79
  686.5 8.4 add_convert_fusion.2
  697.3 46.2 %reduce-scatter.10.cloned.1.call-done = f32[16,512]{1,0:T(8,128)} async-done(((f32[512,512]{1,0:T(8,128)}), f32[16,512]{1,0:T(8,128)}) %reduce-scatter.10.cloned.1.call-update) | async-done | bytes 32784 | tf_op jit(solution)/shard_map/reduce_scatter | solution.py:277
  744.8 5.1 fusion.91
  759.5 38.1 %all-reduce.11 = (f32[512]{0:T(512)S(1)}, f32[512]{0:T(512)S(1)}, f32[512]{0:T(512)S(1)}, f32[512]{0:T(512)S(1)}) all-reduce(f32[512]{0:T(512)S(1)} %get-tuple-element.526, f32[512]{0:T(512)S(1)} %get-tuple-element.621, f32[512]{0:T(512)S(1)} %get-tuple-element.524, ...), channel_id=7, replica_groups=mesh['seq'=8,'head'=4] {'seq','head'}, use_global_device_ids=true, to_apply=%region_25.26.clone | all-reduce | flops 2048 | bytes 16384
  800.0 92.1 %reduce-scatter.14.cloned.1.call-done = f32[64,512]{1,0:T(8,128)} async-done(((f32[2048,512]{1,0:T(8,128)}), f32[64,512]{1,0:T(8,128)}) %reduce-scatter.14.cloned.1.call-update) | async-done | bytes 131088 | tf_op jit(solution)/shard_map/reduce_scatter | solution.py:279
  893.7 146.6 %reduce-scatter.12.cloned.1.call-done = f32[512,64]{0,1:T(8,128)} async-done(((f32[512,2048]{0,1:T(8,128)}), f32[512,64]{0,1:T(8,128)}) %reduce-scatter.12.cloned.1.call-update) | async-done | bytes 131088 | tf_op jit(solution)/shard_map/reduce_scatter | solution.py:278
  1041.8 104.3 %reduce-scatter.8.cloned.1.call-done = f32[16,1536]{1,0:T(8,128)} async-done(((f32[512,1536]{1,0:T(8,128)}), f32[16,1536]{1,0:T(8,128)}) %reduce-scatter.8.cloned.1.call-update) | async-done | bytes 98320 | tf_op jit(solution)/shard_map/reduce_scatter | solution.py:276
  (672 shorter events, 288.1 us)
Async XLA Ops:
  7.2 61.5 %all-gather.4.cloned.1.call-start = ((), (), s32[]{:S(2)}) async-start(), calls=%async_computation.8 | async-start | bytes 1622016 | tf_op jit(solution)/shard_map/all_gather | solution.py:88
  7.9 349.9 %all-gather.6.cloned.1.call-start = ((), (), s32[]{:S(2)}) async-start(), calls=%async_computation.9 | async-start | bytes 2162688 | tf_op jit(solution)/shard_map/all_gather | solution.py:90
  8.7 357.1 %all-gather.8.cloned.1.call-start = ((), (), s32[]{:S(2)}) async-start(), calls=%async_computation.10 | async-start | bytes 2162688 | tf_op jit(solution)/shard_map/all_gather | solution.py:91
  54.3 14.4 %copy-start.18 = (f32[512]{0:T(512)}, f32[512]{0:T(512)S(1)}, u32[]{:S(2)}) copy-start(f32[512]{0:T(512)S(1)} %convert_element_type.110) | copy-start | bytes 6148
  72.1 6.0 copy-start.25
  73.6 39.9 %collective-permute-start.1 = (bf16[1024,384]{1,0:T(8,128)(2,1)}, bf16[1024,384]{1,0:T(8,128)(2,1)}, u32[]{:S(2)}, u32[]{:S(2)}) collective-permute-start(bf16[1024,384]{1,0:T(8,128)(2,1)} %get-tuple-element.612), channel_id=1, source_target_pairs={{0,2},{1,3},{2,0},{3,1},{4,6},{5,7},{6,4},{7,5},{8,10},{9,11},{10,... | collective-permute-start | bytes 2359304 | tf_op jit(solution)/shard_map/ppermute | solution.py:122
  74.4 40.5 %collective-permute-start = (bf16[1024,384]{1,0:T(8,128)(2,1)}, bf16[1024,384]{1,0:T(8,128)(2,1)}, u32[]{:S(2)}, u32[]{:S(2)}) collective-permute-start(bf16[1024,384]{1,0:T(8,128)(2,1)} %get-tuple-element.613), channel_id=1, source_target_pairs={{0,1},{1,0},{2,3},{3,2},{4,5},{5,4},{6,7},{7,6},{8,9},{9,8},{10,11... | collective-permute-start | bytes 2359304 | tf_op jit(solution)/shard_map/ppermute | solution.py:122
  76.4 54.5 %collective-permute-start.2 = (bf16[1024,384]{1,0:T(8,128)(2,1)}, bf16[1024,384]{1,0:T(8,128)(2,1)S(1)}, u32[]{:S(2)}, u32[]{:S(2)}) collective-permute-start(bf16[1024,384]{1,0:T(8,128)(2,1)} %get-tuple-element.611), channel_id=1, source_target_pairs={{0,3},{1,2},{2,1},{3,0},{4,7},{5,6},{6,5},{7,4},{8,11},{9,10},{10,... | collective-permute-start | bytes 2359304 | tf_op jit(solution)/shard_map/ppermute | solution.py:122
  140.9 2.7 copy-start.11
  234.8 24.8 %copy-start.23 = (s32[256]{0:T(256)}, s32[256]{0:T(256)S(1)}, u32[]{:S(2)}) copy-start(s32[256]{0:T(256)S(1)} %get-tuple-element.973) | copy-start | bytes 3076
  234.8 27.6 %copy-start.2 = (bf16[8,4,128,2,64]{2,4,1,3,0:T(8,128)(2,1)}, bf16[8,4,128,2,64]{2,4,1,3,0:T(8,128)(2,1)S(1)}, u32[]{:S(2)}) copy-start(bf16[8,4,128,2,64]{2,4,1,3,0:T(8,128)(2,1)S(1)} %get-tuple-element.943) | copy-start | bytes 3145732
  234.8 27.6 %copy-start.9 = (bf16[8,4,128,2,64]{2,4,1,3,0:T(8,128)(2,1)}, bf16[8,4,128,2,64]{2,4,1,3,0:T(8,128)(2,1)S(1)}, u32[]{:S(2)}) copy-start(bf16[8,4,128,2,64]{2,4,1,3,0:T(8,128)(2,1)S(1)} %get-tuple-element.946) | copy-start | bytes 3145732
  234.8 24.8 %copy-start.22 = (bf16[512]{0:T(512)(128)(2,1)S(1)}, bf16[512]{0:T(512)(128)(2,1)}, u32[]{:S(2)}) copy-start(bf16[512]{0:T(512)(128)(2,1)} %get-tuple-element.587) | copy-start | bytes 3076
  234.8 24.8 %copy-start.21 = (bf16[512]{0:T(512)(128)(2,1)S(1)}, bf16[512]{0:T(512)(128)(2,1)}, u32[]{:S(2)}) copy-start(bf16[512]{0:T(512)(128)(2,1)} %get-tuple-element.586) | copy-start | bytes 3076
  234.8 27.6 %copy-start.17 = (bf16[16,512]{1,0:T(8,128)(2,1)S(1)}, bf16[16,512]{1,0:T(8,128)(2,1)}, u32[]{:S(2)}) copy-start(bf16[16,512]{1,0:T(8,128)(2,1)} %param.20) | copy-start | bytes 49156
  234.8 118.3 %all-to-all-start = ((bf16[4,1024,128]{2,1,0:T(8,128)(2,1)}), bf16[4,1024,128]{2,1,0:T(8,128)(2,1)}, u32[]{:S(2)}, u32[]{:S(2)}) async-start(bf16[4,1024,128]{2,1,0:T(8,128)(2,1)} %bitcast.293), calls=%async_computation | async-start | bytes 2097152 | tf_op jit(solution)/shard_map/all_to_all | solution.py:167
  357.5 26.9 %copy-start = (f32[1024,512]{0,1:T(8,128)}, f32[1024,512]{0,1:T(8,128)S(1)}, u32[]{:S(2)}) copy-start(f32[1024,512]{0,1:T(8,128)S(1)} %get-tuple-element.620) | copy-start | bytes 6291460
  365.7 9.7 copy-start.26
  375.4 3.7 copy-start.28
  388.4 24.6 %all-to-all-start.1 = ((bf16[1024,4,128]{0,2,1:T(8,128)(2,1)}), bf16[1024,4,128]{0,2,1:T(8,128)(2,1)S(1)}, u32[]{:S(2)}, u32[]{:S(2)}) async-start(bf16[1024,4,128]{0,2,1:T(8,128)(2,1)} %bitcast.42), calls=%async_computation.1 | async-start | bytes 2097152 | tf_op jit(solution)/shard_map/all_to_all | solution.py:186
  391.9 179.6 %reduce-scatter.16.cloned.1.call-start = ((), (), s32[]{:S(2)}) async-start(), calls=%async_computation.15 | async-start | bytes 147456
  413.0 4.0 copy-start.3
  413.0 4.1 copy-start.24
  538.1 3.5 copy-start.14
  538.2 205.3 %reduce-scatter.10.cloned.1.call-start = ((), (), s32[]{:S(2)}) async-start(), calls=%async_computation.12 | async-start | bytes 1081344 | tf_op jit(solution)/shard_map/reduce_scatter | solution.py:277
  541.6 350.5 %reduce-scatter.14.cloned.1.call-start = ((), (), s32[]{:S(2)}) async-start(), calls=%async_computation.14 | async-start | bytes 4325376 | tf_op jit(solution)/shard_map/reduce_scatter | solution.py:279
  550.7 489.5 %reduce-scatter.12.cloned.1.call-start = ((), (), s32[]{:S(2)}) async-start(), calls=%async_computation.13 | async-start | bytes 4325376 | tf_op jit(solution)/shard_map/reduce_scatter | solution.py:278
  581.8 4.1 copy-start.10
  599.0 81.9 %copy-start.19 = (f32[512]{0:T(512)S(1)}, f32[512]{0:T(512)}, u32[]{:S(2)}) copy-start(f32[512]{0:T(512)} %copy-done.18) | copy-start | bytes 6148
  599.0 81.9 %all-to-all-start.2 = ((bf16[4,1024,384]{1,2,0:T(8,128)(2,1)}), bf16[4,1024,384]{1,2,0:T(8,128)(2,1)}, u32[]{:S(2)}, u32[]{:S(2)}) async-start(bf16[4,1024,384]{1,2,0:T(8,128)(2,1)} %copy.194), calls=%async_computation.2 | async-start | bytes 6291456 | tf_op jit(solution)/shard_map/all_to_all | solution.py:261
  603.8 542.3 %reduce-scatter.8.cloned.1.call-start = ((), (), s32[]{:S(2)}) async-start(), calls=%async_computation.11 | async-start | bytes 3244032 | tf_op jit(solution)/shard_map/reduce_scatter | solution.py:276
  694.9 50.0 %copy-start.27 = (bf16[512,1536]{1,0:T(8,128)(2,1)S(1)}, bf16[512,1536]{1,0:T(8,128)(2,1)}, u32[]{:S(2)}) copy-start(bf16[512,1536]{1,0:T(8,128)(2,1)} %all-gather.4.cloned.1.call-done) | copy-start | bytes 4718596
  (11 other events, 14.7 us)
Sparse Core Ops, SparseCore 0:
  10.9 57.7 all-gather.3
  71.6 86.4 all-gather.5
  161.1 55.4 all-gather.7
  538.3 33.2 reduce-scatter.15
  573.7 169.7 reduce-scatter.9
  745.6 146.4 reduce-scatter.13
  894.4 145.8 reduce-scatter.11
  1045.7 100.4 reduce-scatter.7
